TPU v7x, 128 devices: a whole 4x4x4 slice. The times are simulated.
128 devices in a mesh: context: 8 (over z, core), tensor: 16 (over x, y).
Axes of the slice: x: 4, y: 4, z: 4, core: 2. Of those that a mesh axis runs over, the one named last changes fastest.
Arguments:
- features: bfloat16 [4096, 3, 8192], P('context', None, 'tensor'), may hold values from -6 to 6
- se_filter: float32 [7, 3, 8192], P(None, None, 'tensor'), may hold values from -1.6 to 1.6
- mr_filter: bfloat16 [128, 512], P(None, 'tensor'), may hold values from -0.61 to 0.61
- stream: bfloat16 [4096, 8192], P('context', 'tensor'), may hold values from -20 to 20
- w_out: bfloat16 [8192, 8192], P('tensor'), may hold values from -0.09375 to 0.09375
- norm_gain: float32 [8192], replicated, may hold values from 0.1 to 1.9
- w_qkv: bfloat16 [8192, 3, 4096], P(None, None, 'tensor'), as said below
Outputs:
- stream_out: bfloat16 [4096, 8192], P('context', 'tensor')
- context_out: bfloat16 [4096, 4096], P('context', 'tensor')
Inputs may be any that keep to these rules, and one draw needn't show every extreme that they name: `w_qkv`: projection weights.
All inputs are finite; a program needn't handle non-finite values.
Results may differ from a plain program's by a relative error of at most 0.019.
Values may be sent and summed in bfloat16 or wider, within the bound.
No kernel may reach another device: no remote copies, remote signals or barrier semaphores. Data moves between devices by JAX's collectives and lax.ppermute only.
A program may use at most 192 MiB of HBM per device.

v0:
```python
import jax
import jax.numpy as jnp
from jax import lax
from jax.sharding import PartitionSpec as P

HD = 128


def passed_along(value, axis, steps):
    count = lax.axis_size(axis)
    initial, last = (max(0, -steps), min(count, count - steps))
    return lax.ppermute(value, axis, [(source, source + steps) for source in range(initial, last)])


def short_filter(padded, se_filter, row_count):
    se_width = se_filter.shape[0]
    filtered = se_filter[0][None] * padded[se_width - 1 : se_width - 1 + row_count].astype(
        jnp.float32
    )
    for offset_lag in range(1, se_width):
        window = padded[se_width - 1 - offset_lag : se_width - 1 - offset_lag + row_count].astype(
            jnp.float32
        )
        filtered = filtered + se_filter[offset_lag][None] * window
    return filtered


def toeplitz_blocks(mr_filter):
    blocks = mr_filter.shape[0]
    groups = mr_filter.shape[1]
    reversed_taps = mr_filter[::-1].T
    period_row = jnp.concatenate([reversed_taps, jnp.zeros((groups, blocks), jnp.bfloat16)], axis=1)
    tiled = jnp.tile(period_row, (1, blocks))[:, : blocks * (2 * blocks - 1)]
    tiled = tiled.reshape(groups, blocks, 2 * blocks - 1)
    return jnp.concatenate([tiled, jnp.zeros((groups, blocks, 1), jnp.bfloat16)], axis=2)


def medium_filter(kv_prev, kv_prod, mr_filter):
    tok_rows, own_chans = kv_prod.shape
    blocks = mr_filter.shape[0]
    groups = mr_filter.shape[1]
    group_width = own_chans // groups
    block_count = tok_rows // blocks
    extended = jnp.concatenate([kv_prev, kv_prod, jnp.zeros((1, own_chans), jnp.bfloat16)], axis=0)
    lower = extended[:tok_rows].reshape(block_count, blocks, groups, group_width)
    upper = extended[blocks : blocks + tok_rows].reshape(block_count, blocks, groups, group_width)
    toeplitz = toeplitz_blocks(mr_filter)
    medium = jnp.einsum(
        "gim,bmgc->bigc", toeplitz[:, :, :blocks], lower, preferred_element_type=jnp.float32
    )
    medium = medium + jnp.einsum(
        "gim,bmgc->bigc", toeplitz[:, :, blocks:], upper, preferred_element_type=jnp.float32
    )
    return medium.reshape(tok_rows, own_chans)


def on_device(features, se_filter, mr_filter, stream, w_out, norm_gain, w_qkv):
    tok_rows = features.shape[0]
    own_chans = features.shape[2]
    se_width = se_filter.shape[0]
    mr_width = mr_filter.shape[0]
    edge_rows = passed_along(features[tok_rows - (se_width - 1) :], "context", 1)
    short_out = short_filter(jnp.concatenate([edge_rows, features], axis=0), se_filter, tok_rows)
    kv_prod = (short_out[:, 1, :] * short_out[:, 2, :]).astype(jnp.bfloat16)
    kv_prev = passed_along(kv_prod[tok_rows - (mr_width - 1) :], "context", 1)
    medium = medium_filter(kv_prev, kv_prod, mr_filter)
    gated = (short_out[:, 0, :] * medium).astype(jnp.bfloat16)
    tensor_rank = lax.axis_index("tensor")
    partial_value = jnp.dot(gated, w_out, preferred_element_type=jnp.float32)
    own_cols = lax.dynamic_slice_in_dim(
        partial_value, tensor_rank * own_chans, own_chans, 1
    ) + stream.astype(jnp.float32)
    term_all = lax.dynamic_update_slice_in_dim(partial_value, own_cols, tensor_rank * own_chans, 1)
    mixed_rows = lax.psum(term_all, "tensor")
    stream_out = lax.dynamic_slice_in_dim(mixed_rows, tensor_rank * own_chans, own_chans, 1).astype(
        jnp.bfloat16
    )
    mean_square = jnp.mean(mixed_rows * mixed_rows, axis=1, keepdims=True)
    normed = (mixed_rows * lax.rsqrt(mean_square + 1e-05) * norm_gain[None, :]).astype(jnp.bfloat16)
    qkv_proj = jnp.einsum("td,dkh->tkh", normed, w_qkv, preferred_element_type=jnp.float32).astype(
        jnp.bfloat16
    )
    head_cols = w_qkv.shape[2]
    head_count = head_cols // HD
    query = qkv_proj[:, 0, :].reshape(tok_rows, head_count, HD)
    position = lax.axis_index("context") * tok_rows + jnp.arange(tok_rows, dtype=jnp.int32)
    scale_factor = HD ** (-0.5)
    run_max = jnp.full((head_count, tok_rows), -1e30, jnp.float32)
    key_block = lax.all_gather(qkv_proj[:, 1, :], "context", axis=0, tiled=True)
    value_block = lax.all_gather(qkv_proj[:, 2, :], "context", axis=0, tiled=True)
    key_count = key_block.shape[0]
    keys_three = key_block.reshape(key_count, head_count, HD)
    values_three = value_block.reshape(key_count, head_count, HD)
    scores = (
        jnp.einsum("qhd,khd->hqk", query, keys_three, preferred_element_type=jnp.float32)
        * scale_factor
    )
    key_position = jnp.arange(key_count, dtype=jnp.int32)
    allowed = key_position[None, :] <= position[:, None]
    scores = jnp.where(allowed[None], scores, -jnp.inf)
    new_max = jnp.maximum(run_max, jnp.max(scores, axis=2))
    expo = jnp.exp(scores - new_max[:, :, None])
    run_total = jnp.sum(expo, axis=2)
    weights = expo.astype(jnp.bfloat16)
    run_acc = jnp.einsum("hqk,khd->hqd", weights, values_three, preferred_element_type=jnp.float32)
    run_max, run_total, run_acc = (new_max, run_total, run_acc)
    result = run_acc / run_total[:, :, None]
    context_out = jnp.transpose(result, (1, 0, 2)).reshape(tok_rows, head_cols).astype(jnp.bfloat16)
    return (stream_out, context_out)


def solution(mesh):
    placed = (
        P("context", None, "tensor"),
        P(None, None, "tensor"),
        P(None, "tensor"),
        P("context", "tensor"),
        P("tensor", None),
        P(),
        P(None, None, "tensor"),
    )
    return jax.shard_map(
        on_device,
        mesh=mesh,
        in_specs=placed,
        out_specs=(P("context", "tensor"), P("context", "tensor")),
        check_vma=False,
    )
```

profile of v0, /device:TPU:1, one launch (start us, length us, event | category | flops | bytes accessed | tf_op | source)
XLA Modules:
  0.0 383.0 jit_solution(14725790758552800340)
XLA Ops:
  8.2 4.9 %collective-permute-start = (bf16[6,3,512]{0,2,1:T(8,128)(2,1)S(1)}, bf16[6,3,512]{0,2,1:T(8,128)(2,1)S(1)}, u32[]{:S(2)}, u32[]{:S(2)}) collective-permute-start(bf16[6,3,512]{0,2,1:T(8,128)(2,1)S(1)} %copy.14), channel_id=1, source_target_pairs={{0,16},{16,32},{32,48},{48,64},{64,80},{80,96},{96,112},{1,17},{17... | collective-permute-start | bytes 55304 | tf_op jit(solution)/shard_map/ppermute | solution.py:12
  15.6 2.6 copy.13
  18.5 1.2 copy.35
  19.8 7.8 %reshape.68 = bf16[32,128,255]{2,1,0:T(8,128)(2,1)} reshape(bf16[32,32640]{1,0:T(8,128)(2,1)S(1)} %slice.124) | data formatting | bytes 4177920 | tf_op jit(solution)/shard_map/reshape | solution.py:34
  28.2 12.6 %multiply_add_fusion = f32[512,3,512]{0,2,1:T(8,128)S(1)} fusion(bf16[512,3,512]{0,2,1:T(8,128)(2,1)} %copy.13, bf16[6,3,512]{0,2,1:T(8,128)(2,1)S(1)} %collective-permute-done, f32[3,512]{1,0:T(4,128)S(1)} %get-tuple-element.20, f32[3,512]{1,0:T(4,128)S(1)} %get-tuple-element.21, f32[3,512]{1,0:T(4,128)} %get-tuple-element.22, ...), kind=kLoop, calls=%fused_computation.19 | loop fusion | flops 29884416 | bytes 4780032 | tf_op jit(solution)/shard_map/add | solution.py:24
  41.1 1.9 collective-permute-start.1
  43.2 1.8 collective-permute-done.1
  44.9 1.5 pad_maximum_fusion.1
  46.4 2.0 reshape.69
  48.4 2.0 reshape.67
  50.4 2.3 fusion.24
  54.0 11.6 %fusion.34 = f32[512,8192]{1,0:T(8,128)} fusion(bf16[512,8192]{1,0:T(8,128)(2,1)} %param.11, f32[64,8,4,128]{3,2,1,0:T(4,128)S(1)} %bitcast.73, f32[512,3,512]{0,2,1:T(8,128)S(1)} %multiply_add_fusion), kind=kOutput, calls=%fused_computation.49 | convolution fusion | flops 4295491584 | bytes 27262976 | tf_op jit(solution)/shard_map/dot_general | solution.py:69
  65.6 2.4 add_dynamic-update-slice_fusion
  68.2 222.7 %all-reduce.5.cloned.1.call-done = f32[512,8192]{1,0:T(8,128)} async-done(((f32[512,8192]{1,0:T(8,128)}), f32[512,8192]{1,0:T(8,128)}) %all-reduce.5.cloned.1.call-update) | async-done | bytes 16777232 | tf_op jit(solution)/shard_map/psum | solution.py:74
  290.9 7.0 %multiply_reduce_fusion = f32[512]{0:T(512)S(1)} fusion(f32[512,8192]{1,0:T(8,128)} %all-reduce.5.cloned.1.call-done), kind=kLoop, calls=%fused_computation.3 | loop fusion | flops 8388096 | bytes 16779264 | tf_op jit(solution)/shard_map/reduce_sum | solution.py:78
  297.9 14.8 %fusion.16 = bf16[512,3,256]{0,2,1:T(8,128)(2,1)S(1)} fusion(bf16[8192,3,256]{2,0,1:T(8,128)(2,1)} %param.13, f32[512,8192]{1,0:T(8,128)} %all-reduce.5.cloned.1.call-done, f32[8192]{0:T(1024)S(1)} %copy-done.5, f32[512]{0:T(512)S(1)} %add_rsqrt_fusion), kind=kOutput, calls=%fused_computation.32 | convolution fusion | flops 6455427072 | bytes 30181376 | tf_op jit(solution)/shard_map/td,dkh->tkh/dot_general | solution.py:80
  314.3 1.7 iota_compare_fusion
  316.0 2.1 dynamic-slice_convert_fusion
  318.1 21.7 %all-gather.5.cloned.1.call-done = bf16[4096,1,256]{0,2,1:T(8,128)(2,1)} async-done(((bf16[512,1,256]{0,2,1:T(8,128)(2,1)}), bf16[4096,1,256]{0,2,1:T(8,128)(2,1)}) %all-gather.5.cloned.1.call-update) | async-done | bytes 2097168 | tf_op jit(solution)/shard_map/all_gather | solution.py:89
  339.7 5.3 %fusion = (f32[2,512]{1,0:T(2,128)S(1)}, f32[2,512,4096]{2,1,0:T(8,128)S(1)}) fusion(pred[512,4096]{1,0:T(8,128)(4,1)S(1)} %iota_compare_fusion, bf16[512,2,128]{0,2,1:T(8,128)(2,1)S(1)} %bitcast.77, bf16[4096,2,128]{0,2,1:T(8,128)(2,1)} %bitcast.81), kind=kOutput, calls=%fused_computation.4 | convolution fusion | flops 1086323712 | bytes 21237760 | tf_op jit(solution)/shard_map/qhd,khd->hqk/dot_general | solution.py:95
  345.1 5.7 %copy-done = f32[2,512,4096]{2,1,0:T(8,128)} copy-done((f32[2,512,4096]{2,1,0:T(8,128)}, f32[2,512,4096]{2,1,0:T(8,128)S(1)}, u32[]{:S(2)}) %copy-start) | copy-done | bytes 16777240
  350.8 4.6 %fusion.1 = f32[2,512]{1,0:T(2,128)S(1)} fusion(f32[2,512,4096]{2,1,0:T(8,128)S(1)} %get-tuple-element.19, f32[2,512]{1,0:T(2,128)S(1)} %broadcast_maximum_fusion, pred[512,4096]{1,0:T(8,128)(4,1)S(1)} %iota_compare_fusion), kind=kLoop, calls=%fused_computation.5 | loop fusion | flops 16776192 | bytes 18882560 | tf_op jit(solution)/shard_map/reduce_sum | solution.py:103
  355.4 11.9 %all-gather.7.cloned.1.call-done = bf16[4096,1,256]{0,2,1:T(8,128)(2,1)} async-done(((bf16[512,1,256]{0,2,1:T(8,128)(2,1)}), bf16[4096,1,256]{0,2,1:T(8,128)(2,1)}) %all-gather.7.cloned.1.call-update) | async-done | bytes 2097168 | tf_op jit(solution)/shard_map/all_gather | solution.py:90
  367.2 8.4 %fusion.31 = bf16[512,2,128]{0,2,1:T(8,128)(2,1)S(1)} fusion(bf16[4096,2,128]{0,2,1:T(8,128)(2,1)} %bitcast.82, f32[2,512,4096]{2,1,0:T(8,128)} %copy-done, f32[2,512]{1,0:T(2,128)S(1)} %broadcast_maximum_fusion, pred[512,4096]{1,0:T(8,128)(4,1)S(1)} %iota_compare_fusion, f32[512,2]{0,1:T(2,128)S(1)} %bitcast.80), kind=kOutput, calls=%fused_computation.47 | convolution fusion | flops 1090781184 | bytes 21241856 | tf_op jit(solution)/shard_map/hqk,khd->hqd/dot_general | solution.py:105
  (39 shorter events, 8.8 us)
Async XLA Ops:
  7.2 11.1 %copy-start.4 = (bf16[128,32]{0,1:T(8,128)(2,1)S(1)}, bf16[128,32]{0,1:T(8,128)(2,1)}, u32[]{:S(2)}) copy-start(bf16[128,32]{0,1:T(8,128)(2,1)} %param.9) | copy-start | bytes 24580
  7.2 283.8 %all-reduce.5.cloned.1.call-start = ((), (), s32[]{:S(2)}) async-start(), calls=%async_computation | async-start | bytes 33554432 | tf_op jit(solution)/shard_map/psum | solution.py:74
  8.2 20.0 %collective-permute-start = (bf16[6,3,512]{0,2,1:T(8,128)(2,1)S(1)}, bf16[6,3,512]{0,2,1:T(8,128)(2,1)S(1)}, u32[]{:S(2)}, u32[]{:S(2)}) collective-permute-start(bf16[6,3,512]{0,2,1:T(8,128)(2,1)S(1)} %copy.14), channel_id=1, source_target_pairs={{0,16},{16,32},{32,48},{48,64},{64,80},{80,96},{96,112},{1,17},{17... | collective-permute-start | bytes 55304 | tf_op jit(solution)/shard_map/ppermute | solution.py:12
  41.1 3.9 %collective-permute-start.1 = (bf16[127,512]{0,1:T(8,128)(2,1)S(1)}, bf16[127,512]{0,1:T(8,128)(2,1)S(1)}, u32[]{:S(2)}, u32[]{:S(2)}) collective-permute-start(bf16[127,512]{0,1:T(8,128)(2,1)S(1)} %slice_bitcast_fusion.3), channel_id=1, source_target_pairs={{0,16},{16,32},{32,48},{48,64},{64,80},{80,96},{96,112},{1,17},{17... | collective-permute-start | bytes 390152 | tf_op jit(solution)/shard_map/ppermute | solution.py:12
  50.4 2.3 copy-start.1
  50.4 2.4 copy-start.2
  54.0 11.6 %copy-start.3 = (bf16[512,512]{1,0:T(8,128)(2,1)S(1)}, bf16[512,512]{1,0:T(8,128)(2,1)}, u32[]{:S(2)}) copy-start(bf16[512,512]{1,0:T(8,128)(2,1)} %param.10) | copy-start | bytes 1572868
  68.0 229.9 %copy-start.5 = (f32[8192]{0:T(1024)S(1)}, f32[8192]{0:T(1024)}, u32[]{:S(2)}) copy-start(f32[8192]{0:T(1024)} %param.12) | copy-start | bytes 98308
  68.0 271.8 %all-gather.5.cloned.1.call-start = ((), (), s32[]{:S(2)}) async-start(), calls=%async_computation.1 | async-start | bytes 2359296 | tf_op jit(solution)/shard_map/all_gather | solution.py:89
  313.6 53.7 %all-gather.7.cloned.1.call-start = ((), (), s32[]{:S(2)}) async-start(), calls=%async_computation.2 | async-start | bytes 2359296 | tf_op jit(solution)/shard_map/all_gather | solution.py:90
  345.0 5.7 %copy-start = (f32[2,512,4096]{2,1,0:T(8,128)}, f32[2,512,4096]{2,1,0:T(8,128)S(1)}, u32[]{:S(2)}) copy-start(f32[2,512,4096]{2,1,0:T(8,128)S(1)} %get-tuple-element.19) | copy-start | bytes 50331652
Sparse Core Ops, SparseCore 0:
  68.1 222.7 all-reduce.4
  313.7 26.0 all-gather.4
  341.4 25.7 all-gather.6
where the time goes:
time: 384 us; the launch traced here: 383 us
  waiting for transfers between devices  259 us (67%)
  matrix products  43.2 us (11%)
  local copies, waits for them, and re-layouts  30 us (8%)
  other arithmetic  30 us (8%)
  between operations  13.9 us (4%)
  starting transfers between devices  7.16 us (2%)
    psum x1, waiting for transfers between devices, on_device(): mixed_rows = lax.psum(term_all, 'tensor')  223 us
    all_gather x1, waiting for transfers between devices, on_device(): key_block = lax.all_gather(qkv_proj[:, 1, :], 'context', axis=0, tiled=True)  21.7 us
    dot_general x1, matrix products, on_device(): jnp.einsum('td,dkh->tkh', normed, w_qkv, preferred_element_type=jnp.float32)  14.8 us
    add x1, other arithmetic, short_filter(): filtered = filtered + se_filter[offset_lag][None] * window  12.6 us
    unnamed x19, local copies, waits for them, and re-layouts  12.2 us
    all_gather x1, waiting for transfers between devices, on_device(): lax.all_gather(qkv_proj[:, 2, :], 'context', axis=0, tiled=True)  11.9 us
    dot_general x1, matrix products, on_device(): partial_value = jnp.dot(gated, w_out, preferred_element_type=jnp.float32)  11.6 us
    dot_general x1, matrix products, on_device(): jnp.einsum('hqk,khd->hqd', weights, values_three, preferred_element_type=...  8.42 us
  transfers between devices with their start and end apart: 5, of which 4 were waited for; matrix products, arithmetic and copies ran while one was open for 8% of the time, Pallas kernels for 0%

commit v1 on v0

--- a/solution.py
+++ b/solution.py
@@ -2,6 +2,7 @@
 import jax.numpy as jnp
 from jax import lax
 from jax.sharding import PartitionSpec as P
+from jax.lax import all_to_all, axis_size
 
 HD = 128
 
@@ -55,6 +56,19 @@
 
 
 def on_device(features, se_filter, mr_filter, stream, w_out, norm_gain, w_qkv):
+
+    def feed_outputs_here(local_array, where_dim):
+        v_next = jnp.concatenate(
+            all_to_all(
+                jnp.stack([local_array] * axis_size("context"), 0),
+                "context",
+                split_axis=0,
+                concat_axis=0,
+            ),
+            where_dim,
+        )
+        return v_next
+
     tok_rows = features.shape[0]
     own_chans = features.shape[2]
     se_width = se_filter.shape[0]
@@ -87,7 +101,7 @@
     scale_factor = HD ** (-0.5)
     run_max = jnp.full((head_count, tok_rows), -1e30, jnp.float32)
     key_block = lax.all_gather(qkv_proj[:, 1, :], "context", axis=0, tiled=True)
-    value_block = lax.all_gather(qkv_proj[:, 2, :], "context", axis=0, tiled=True)
+    value_block = feed_outputs_here(qkv_proj[:, 2, :], 0)
     key_count = key_block.shape[0]
     keys_three = key_block.reshape(key_count, head_count, HD)
     values_three = value_block.reshape(key_count, head_count, HD)

time: 384 us -> 389 us (1.013)
  starting transfers between devices: 7.16 us -> 12.6 us
  local copies, waits for them, and re-layouts: 30 us -> 34 us
    all_to_all x0 -> x1, waiting for transfers between devices: none -> 31.1 us  [feed_outputs_here(): all_to_all(jnp.stack([local_array] * axis_size('context'), 0), 'context',...]
    all_gather x1, waiting for transfers between devices: 21.7 us -> 0.01 us  [on_device(): key_block = lax.all_gather(qkv_proj[:, 1, :], 'context', axis=0, tiled=True)]
    all_gather x1 -> x0, waiting for transfers between devices: 11.9 us -> none  [on_device(): lax.all_gather(qkv_proj[:, 2, :], 'context', axis=0, tiled=True)]
    unnamed x19 -> x17, local copies, waits for them, and re-layouts: 12.2 us -> 6.5 us
    another operation x0 -> x2, local copies, waits for them, and re-layouts: none -> 5.7 us  [the longest x1 4.19 us: on_device(): values_three = value_block.reshape(key_count, head_count, HD)]
    all_to_all x0 -> x1, starting transfers between devices: none -> 5.51 us  [feed_outputs_here(): all_to_all(jnp.stack([local_array] * axis_size('context'), 0), 'context',...]
    all_to_all x0 -> x1, local copies, waits for them, and re-layouts: none -> 4.09 us  [feed_outputs_here(): all_to_all(jnp.stack([local_array] * axis_size('context'), 0), 'context',...]
  transfers between devices with their start and end apart: 5 -> 5, of which waited for: 4 -> 3; matrix products, arithmetic and copies ran while one was open for 8% -> 7% of each run, Pallas kernels for 0% -> 0%
where the time goes in v1:
time: 389 us; the launch traced here: 388 us
  waiting for transfers between devices  256 us (66%)
  matrix products  41.6 us (11%)
  local copies, waits for them, and re-layouts  34 us (9%)
  other arithmetic  30 us (8%)
  between operations  14.2 us (4%)
  starting transfers between devices  12.6 us (3%)
    psum x1, waiting for transfers between devices, on_device(): mixed_rows = lax.psum(term_all, 'tensor')  223 us
    all_to_all x1, waiting for transfers between devices, feed_outputs_here(): all_to_all(jnp.stack([local_array] * axis_size('context'), 0), 'context',...  31.1 us
    dot_general x1, matrix products, on_device(): jnp.einsum('td,dkh->tkh', normed, w_qkv, preferred_element_type=jnp.float32)  14.8 us
    add x1, other arithmetic, short_filter(): filtered = filtered + se_filter[offset_lag][None] * window  12.6 us
    dot_general x1, matrix products, on_device(): partial_value = jnp.dot(gated, w_out, preferred_element_type=jnp.float32)  11.6 us
    reshape x1, local copies, waits for them, and re-layouts, toeplitz_blocks(): tiled = tiled.reshape(groups, blocks, 2 * blocks - 1)  7.8 us
  transfers between devices with their start and end apart: 5, of which 3 were waited for; matrix products, arithmetic and copies ran while one was open for 7% of the time, Pallas kernels for 0%

profile of v1, /device:TPU:1, one launch (start us, length us, event | category | flops | bytes accessed | tf_op | source)
XLA Modules:
  0.0 387.9 jit_solution(4583615009603778252)
XLA Ops:
  8.2 4.9 %collective-permute-start = (bf16[6,3,512]{0,2,1:T(8,128)(2,1)S(1)}, bf16[6,3,512]{0,2,1:T(8,128)(2,1)S(1)}, u32[]{:S(2)}, u32[]{:S(2)}) collective-permute-start(bf16[6,3,512]{0,2,1:T(8,128)(2,1)S(1)} %copy.24), channel_id=1, source_target_pairs={{0,16},{16,32},{32,48},{48,64},{64,80},{80,96},{96,112},{1,17},{17... | collective-permute-start | bytes 55304 | tf_op jit(solution)/shard_map/ppermute | solution.py:13
  15.6 2.6 copy.23
  19.8 7.8 %reshape.67 = bf16[32,128,255]{2,1,0:T(8,128)(2,1)} reshape(bf16[32,32640]{1,0:T(8,128)(2,1)S(1)} %slice.124) | data formatting | bytes 4177920 | tf_op jit(solution)/shard_map/reshape | solution.py:35
  28.2 12.6 %multiply_add_fusion = f32[512,3,512]{0,2,1:T(8,128)S(1)} fusion(bf16[512,3,512]{0,2,1:T(8,128)(2,1)} %copy.23, bf16[6,3,512]{0,2,1:T(8,128)(2,1)S(1)} %collective-permute-done, f32[3,512]{1,0:T(4,128)S(1)} %get-tuple-element.22, f32[3,512]{1,0:T(4,128)S(1)} %get-tuple-element.23, f32[3,512]{1,0:T(4,128)} %get-tuple-element.24, ...), kind=kLoop, calls=%fused_computation.19 | loop fusion | flops 29884416 | bytes 4780032 | tf_op jit(solution)/shard_map/add | solution.py:25
  41.1 1.9 collective-permute-start.1
  43.2 1.8 collective-permute-done.1
  46.4 2.0 reshape.68
  48.3 2.0 reshape.66
  50.3 2.3 fusion.24
  53.9 11.6 %fusion.34 = f32[512,8192]{1,0:T(8,128)} fusion(bf16[512,8192]{1,0:T(8,128)(2,1)} %param.11, f32[64,8,4,128]{3,2,1,0:T(4,128)S(1)} %bitcast.76, f32[512,3,512]{0,2,1:T(8,128)S(1)} %multiply_add_fusion), kind=kOutput, calls=%fused_computation.49 | convolution fusion | flops 4295491584 | bytes 27262976 | tf_op jit(solution)/shard_map/dot_general | solution.py:83
  65.5 2.4 add_dynamic-update-slice_fusion
  68.2 222.7 %all-reduce.5.cloned.1.call-done = f32[512,8192]{1,0:T(8,128)} async-done(((f32[512,8192]{1,0:T(8,128)}), f32[512,8192]{1,0:T(8,128)}) %all-reduce.5.cloned.1.call-update) | async-done | bytes 16777232 | tf_op jit(solution)/shard_map/psum | solution.py:88
  290.8 7.0 %multiply_reduce_fusion = f32[512]{0:T(512)S(1)} fusion(f32[512,8192]{1,0:T(8,128)} %all-reduce.5.cloned.1.call-done), kind=kLoop, calls=%fused_computation.3 | loop fusion | flops 8388096 | bytes 16779264 | tf_op jit(solution)/shard_map/reduce_sum | solution.py:92
  297.8 14.8 %fusion.16 = bf16[512,3,256]{0,2,1:T(8,128)(2,1)S(1)} fusion(bf16[8192,3,256]{2,0,1:T(8,128)(2,1)} %param.13, f32[512,8192]{1,0:T(8,128)} %all-reduce.5.cloned.1.call-done, f32[8192]{0:T(1024)S(1)} %copy-done.4, f32[512]{0:T(512)S(1)} %add_rsqrt_fusion), kind=kOutput, calls=%fused_computation.32 | convolution fusion | flops 6455427072 | bytes 30181376 | tf_op jit(solution)/shard_map/td,dkh->tkh/dot_general | solution.py:94
  313.4 1.5 stack.3
  314.9 5.5 %all-to-all-start = ((bf16[8,512,256]{1,2,0:T(8,128)(2,1)}), bf16[8,512,256]{1,2,0:T(8,128)(2,1)}, u32[]{:S(2)}, u32[]{:S(2)}) async-start(bf16[8,512,256]{1,2,0:T(8,128)(2,1)} %stack.3), calls=%async_computation | async-start | bytes 4194304 | tf_op jit(solution)/shard_map/all_to_all | solution.py:62
  320.4 1.7 iota_compare_fusion
  322.1 2.1 dynamic-slice_convert_fusion
  324.2 31.1 %all-to-all-done = bf16[8,512,256]{1,2,0:T(8,128)(2,1)} async-done(((bf16[8,512,256]{1,2,0:T(8,128)(2,1)}), bf16[8,512,256]{1,2,0:T(8,128)(2,1)}, u32[]{:S(2)}, u32[]{:S(2)}) %all-to-all-start) | async-done | bytes 2097184 | tf_op jit(solution)/shard_map/all_to_all | solution.py:62
  355.3 4.1 %copy.32 = bf16[8,512,256]{1,0,2:T(8,128)(2,1)} copy(bf16[8,512,256]{1,2,0:T(8,128)(2,1)} %all-to-all-done) | data formatting | bytes 4194304 | tf_op jit(solution)/shard_map/all_to_all | solution.py:62
  359.4 4.2 %reshape_reshape.3 = bf16[4096,2,128]{0,2,1:T(8,128)(2,1)} reshape(bf16[8,512,256]{1,0,2:T(8,128)(2,1)} %copy.32) | data formatting | bytes 4194304 | tf_op jit(solution)/shard_map/reshape;reshape | solution.py:107
  363.6 5.3 %fusion = (f32[2,512]{1,0:T(2,128)S(1)}, f32[2,512,4096]{2,1,0:T(8,128)S(1)}) fusion(pred[512,4096]{1,0:T(8,128)(4,1)S(1)} %iota_compare_fusion, bf16[512,2,128]{0,2,1:T(8,128)(2,1)S(1)} %bitcast.80, bf16[4096,2,128]{0,2,1:T(8,128)(2,1)} %bitcast.84), kind=kOutput, calls=%fused_computation.4 | convolution fusion | flops 1086323712 | bytes 21237760 | tf_op jit(solution)/shard_map/qhd,khd->hqk/dot_general | solution.py:109
  368.9 4.6 %fusion.1 = f32[2,512]{1,0:T(2,128)S(1)} fusion(f32[2,512,4096]{2,1,0:T(8,128)S(1)} %get-tuple-element.21, f32[2,512]{1,0:T(2,128)S(1)} %broadcast_maximum_fusion, pred[512,4096]{1,0:T(8,128)(4,1)S(1)} %iota_compare_fusion), kind=kLoop, calls=%fused_computation.5 | loop fusion | flops 16776192 | bytes 18882560 | tf_op jit(solution)/shard_map/reduce_sum | solution.py:117
  373.6 6.7 %fusion.31 = bf16[512,2,128]{0,2,1:T(8,128)(2,1)S(1)} fusion(bf16[4096,2,128]{0,2,1:T(8,128)(2,1)} %reshape_reshape.3, f32[2,512,4096]{2,1,0:T(8,128)S(1)} %get-tuple-element.21, f32[2,512]{1,0:T(2,128)S(1)} %broadcast_maximum_fusion, pred[512,4096]{1,0:T(8,128)(4,1)S(1)} %iota_compare_fusion, f32[512,2]{0,1:T(2,128)S(1)} %bitcast.83), kind=kOutput, calls=%fused_computation.47 | convolution fusion | flops 1090781184 | bytes 21241856 | tf_op jit(solution)/shard_map/hqk,khd->hqd/dot_general | solution.py:119
  (39 shorter events, 10.7 us)
Async XLA Ops:
  7.2 11.0 %copy-start.3 = (bf16[128,32]{0,1:T(8,128)(2,1)S(1)}, bf16[128,32]{0,1:T(8,128)(2,1)}, u32[]{:S(2)}) copy-start(bf16[128,32]{0,1:T(8,128)(2,1)} %param.9) | copy-start | bytes 24580
  7.2 283.7 %all-reduce.5.cloned.1.call-start = ((), (), s32[]{:S(2)}) async-start(), calls=%async_computation.1 | async-start | bytes 33554432 | tf_op jit(solution)/shard_map/psum | solution.py:88
  8.2 20.0 %collective-permute-start = (bf16[6,3,512]{0,2,1:T(8,128)(2,1)S(1)}, bf16[6,3,512]{0,2,1:T(8,128)(2,1)S(1)}, u32[]{:S(2)}, u32[]{:S(2)}) collective-permute-start(bf16[6,3,512]{0,2,1:T(8,128)(2,1)S(1)} %copy.24), channel_id=1, source_target_pairs={{0,16},{16,32},{32,48},{48,64},{64,80},{80,96},{96,112},{1,17},{17... | collective-permute-start | bytes 55304 | tf_op jit(solution)/shard_map/ppermute | solution.py:13
  41.1 3.9 collective-permute-start.1
  50.3 2.3 copy-start
  50.3 2.4 copy-start.1
  53.9 11.6 %copy-start.2 = (bf16[512,512]{1,0:T(8,128)(2,1)S(1)}, bf16[512,512]{1,0:T(8,128)(2,1)}, u32[]{:S(2)}) copy-start(bf16[512,512]{1,0:T(8,128)(2,1)} %param.10) | copy-start | bytes 1572868
  67.9 229.9 %copy-start.4 = (f32[8192]{0:T(1024)S(1)}, f32[8192]{0:T(1024)}, u32[]{:S(2)}) copy-start(f32[8192]{0:T(1024)} %param.12) | copy-start | bytes 98308
  67.9 295.6 %all-gather.3.cloned.1.call-start = ((), (), s32[]{:S(2)}) async-start(), calls=%async_computation.2 | async-start | bytes 2359296 | tf_op jit(solution)/shard_map/all_gather | solution.py:103
  314.9 40.4 %all-to-all-start = ((bf16[8,512,256]{1,2,0:T(8,128)(2,1)}), bf16[8,512,256]{1,2,0:T(8,128)(2,1)}, u32[]{:S(2)}, u32[]{:S(2)}) async-start(bf16[8,512,256]{1,2,0:T(8,128)(2,1)} %stack.3), calls=%async_computation | async-start | bytes 4194304 | tf_op jit(solution)/shard_map/all_to_all | solution.py:62
Sparse Core Ops, SparseCore 0:
  68.1 222.7 all-reduce.4
  313.5 34.7 all-gather.2
